TPU v7x, 32 devices: a whole 2x2x4 slice. The times are simulated.
32 devices in a mesh: loop: 8 (over z, x), rep: 4 (over y, core).
Axes of the slice: x: 2, y: 2, z: 4, core: 2. Of those that a mesh axis runs over, the one named last changes fastest.
Arguments:
- features: float32 [4096, 128], P('loop'), may hold values from -6 to 6
- weight: float32 [128, 256], replicated, may hold values from -0.5 to 0.5
- bias: float32 [256], replicated, may hold values from -3 to 3
- tile_values: float32 [512, 128, 128], P(('loop', 'rep')), may hold values from -0.125 to 0.125
- tile_rows: int32 [512], P(('loop', 'rep')), may hold values from 0 to 31, as said below
- tile_cols: int32 [512], P(('loop', 'rep')), may hold values from 0 to 31, as said below
- tile_count: int32 [32], P(('loop', 'rep')), may hold values from 1 to 16, as said below
- cotangent: float32 [4096, 256], P('loop'), may hold values from -0.6 to 0.6
Outputs:
- output: float32 [4096, 256], P('loop')
- grad_features: float32 [4096, 128], P('loop')
- grad_weight: float32 [128, 256], replicated
- grad_bias: float32 [256], replicated
Inputs may be any that keep to these rules, and one draw needn't show every extreme that they name: `tile_rows`: every slot of a device at loop index l names a row block from l * 4 to (l + 1) * 4 - 1. `tile_cols`: for every loop index m, the live slots of one device name at most 2 different column blocks from m * 4 to (m + 1) * 4 - 1; for every loop index some device names exactly 2 of one such range. `tile_count`: for every loop index some device has all 16 slots live.
All inputs are finite; a program needn't handle non-finite values.
Results may differ from a plain program's by a relative error of at most 0.0001.
Values sent between devices are 32-bit elements; how exact they have to be, the bound alone decides.
No kernel may reach another device: no remote copies, remote signals or barrier semaphores. Data moves between devices by JAX's collectives and lax.ppermute only.
A program may use at most 64 MiB of HBM per device.

v0:
```python
import jax
import jax.numpy as jnp
from jax import lax
from jax.sharding import PartitionSpec as P


def per_device(features, weight, bias, tile_values, tile_rows, tile_cols, tile_count, cotangent):
    highest = lax.Precision.HIGHEST
    tile_side = tile_values.shape[1]
    rows_here = features.shape[0]
    nblocks = rows_here // tile_side
    slots = tile_values.shape[0]
    local_rows = tile_rows - lax.axis_index("loop") * nblocks
    live_slot = (jnp.arange(slots, dtype=jnp.int32) < tile_count[0]).astype(jnp.float32)
    row_pick = (local_rows[:, None] == jnp.arange(nblocks, dtype=jnp.int32)[None, :]).astype(
        jnp.float32
    )
    row_pick = row_pick * live_slot[:, None]
    gathered = lax.all_gather(features, "loop", axis=0, tiled=True)
    width = gathered.shape[1]
    blocks = gathered.reshape(-1, tile_side, width)[tile_cols]
    products = jnp.einsum("kij,kjf->kif", tile_values, blocks, precision=highest)
    aggregated = lax.psum(
        jnp.einsum("kb,kif->bif", row_pick, products, precision=highest), "rep"
    ).reshape(rows_here, -1)
    preactive = jnp.dot(aggregated, weight, precision=highest) + bias
    logistic = jax.nn.sigmoid(preactive)
    output = preactive * logistic
    gradient = cotangent * logistic * (1.0 + preactive * (1.0 - logistic))
    spread = jnp.dot(gradient, weight.T, precision=highest)
    source_blocks = spread.reshape(nblocks, tile_side, spread.shape[1])[
        jnp.clip(local_rows, 0, nblocks - 1)
    ]
    outgoing = jnp.einsum("kji,kjf->kif", tile_values, source_blocks, precision=highest)
    outgoing = outgoing * live_slot[:, None, None]
    span = rows_here * lax.axis_size("loop") // tile_side + 2
    column_pick = (tile_cols[:, None] == jnp.arange(span, dtype=jnp.int32)[None, :]).astype(
        jnp.float32
    )
    placed = jnp.einsum("kb,kif->bif", column_pick, outgoing, precision=highest)
    placed = placed.reshape(span * tile_side, outgoing.shape[2])
    term = lax.psum_scatter(
        lax.slice_in_dim(placed, 0, rows_here * lax.axis_size("loop"), axis=0),
        "loop",
        scatter_dimension=0,
        tiled=True,
    )
    own_rows = lax.psum(term, "rep")
    weight_term = jnp.dot(aggregated.T, gradient, precision=highest)
    bias_term = jnp.sum(gradient, axis=0)
    grad_weight, grad_bias = lax.psum((weight_term, bias_term), "loop")
    return (output, own_rows, grad_weight, grad_bias)


def solution(mesh):
    return jax.shard_map(
        per_device,
        mesh=mesh,
        in_specs=(
            P("loop", None),
            P(),
            P(),
            P(("loop", "rep"), None, None),
            P(("loop", "rep")),
            P(("loop", "rep")),
            P(("loop", "rep")),
            P("loop", None),
        ),
        out_specs=(P("loop", None), P("loop", None), P(), P()),
        check_vma=False,
    )
```

profile of v0, /device:TPU:0, one launch (start us, length us, event | category | flops | bytes accessed | tf_op | source)
XLA Modules:
  0.0 293.9 jit_solution(1856292996977088046)
XLA Ops:
  7.2 0.0 copy-start
  7.2 0.0 all-gather.2.cloned.1.call-start
  7.2 0.7 all-gather.2.cloned.1.call-update
  7.9 0.0 all-reduce.4.cloned.1.call-start
  8.6 0.7 compare_select_fusion.1
  9.3 0.7 compare_select_fusion
  10.0 52.0 %all-gather.2.cloned.1.call-done = f32[4096,128]{1,0:T(8,128)} async-done(((f32[512,128]{1,0:T(8,128)}), f32[4096,128]{1,0:T(8,128)}) %all-gather.2.cloned.1.call-update) | async-done | bytes 2097168 | tf_op jit(solution)/shard_map/all_gather | solution.py:19
  62.0 2.2 gather_fusion
  64.2 0.0 copy-done
  64.2 1.8 fusion.16
  66.0 0.0 copy-start.5
  66.0 0.0 copy-start.4
  66.0 0.0 copy-start.7
  66.1 0.5 copy.14
  66.6 0.0 copy-start.6
  66.6 0.6 fusion.2
  67.2 0.7 copy.12
  67.9 0.0 all-reduce.4.cloned.1.call-update
  68.0 0.0 reduce-scatter.2.cloned.1.call-start
  68.0 0.0 copy-done.5
  68.0 0.1 fusion.7
  68.1 30.8 %all-reduce.4.cloned.1.call-done = f32[512,128]{1,0:T(8,128)} async-done(((f32[512,128]{1,0:T(8,128)}), f32[512,128]{1,0:T(8,128)}) %all-reduce.4.cloned.1.call-update) | async-done | bytes 262160 | tf_op jit(solution)/shard_map/psum | solution.py:23
  98.9 0.0 copy-done.4
  98.9 0.0 copy-done.7
  98.9 0.0 copy-done.6
  98.9 2.5 fusion.15
  101.4 0.0 copy-start.1
  101.4 0.6 fusion.17
  102.0 0.2 copy-done.1
  102.2 0.6 gather_fusion.1
  102.8 1.8 fusion.18
  104.7 0.5 copy.15
  105.2 1.0 fusion
  106.2 2.6 copy.13
  108.8 0.0 reduce-scatter.2.cloned.1.call-update
  108.8 0.0 all-reduce.8.cloned.1.call-start
  108.9 1.0 copy-done.2
  109.8 0.1 copy-done.3
  109.9 1.3 fusion.19
  111.2 0.0 all-reduce.8.cloned.1.call-update
  111.2 0.0 all-reduce.6.cloned.1.call-start
  111.3 66.0 %reduce-scatter.2.cloned.1.call-done = f32[512,128]{1,0:T(8,128)} async-done(((f32[4096,128]{1,0:T(8,128)}), f32[512,128]{1,0:T(8,128)}) %reduce-scatter.2.cloned.1.call-update) | async-done | bytes 262160 | tf_op jit(solution)/shard_map/reduce_scatter | solution.py:42
  177.3 0.0 all-reduce.6.cloned.1.call-update
  177.3 19.7 %psum.31 = f32[256]{0:T(256)} all-reduce(f32[256]{0:T(256)S(1)} %get-tuple-element.4), channel_id=1, replica_groups=mesh['loop'=8,'rep'=4] {'loop'}, use_global_device_ids=true, to_apply=%region_5.6 | all-reduce | flops 256 | bytes 2048 | tf_op jit(solution)/shard_map/psum | solution.py:51
  197.0 53.6 %all-reduce.8.cloned.1.call-done = f32[128,256]{1,0:T(8,128)} async-done(((f32[128,256]{1,0:T(8,128)}), f32[128,256]{1,0:T(8,128)}) %all-reduce.8.cloned.1.call-update) | async-done | bytes 131088 | tf_op jit(solution)/shard_map/psum | solution.py:51
  250.6 33.6 %all-reduce.6.cloned.1.call-done = f32[512,128]{1,0:T(8,128)} async-done(((f32[512,128]{1,0:T(8,128)}), f32[512,128]{1,0:T(8,128)}) %all-reduce.6.cloned.1.call-update) | async-done | bytes 262160 | tf_op jit(solution)/shard_map/psum | solution.py:48
  284.2 1.7 copy.20
  285.8 1.6 copy.21
  (5 shorter events, 0.0 us)
Async XLA Ops:
  7.2 57.0 %copy-start = (f32[16,128,128]{2,1,0:T(8,128)S(1)}, f32[16,128,128]{2,1,0:T(8,128)}, u32[]{:S(2)}) copy-start(f32[16,128,128]{2,1,0:T(8,128)} %param.11) | copy-start | bytes 3145732
  7.2 54.8 %all-gather.2.cloned.1.call-start = ((), (), s32[]{:S(2)}) async-start(), calls=%async_computation.1 | async-start | bytes 2359296 | tf_op jit(solution)/shard_map/all_gather | solution.py:19
  7.9 91.0 %all-reduce.4.cloned.1.call-start = ((), (), s32[]{:S(2)}) async-start(), calls=%async_computation.2 | async-start | bytes 524288 | tf_op jit(solution)/shard_map/psum | solution.py:23
  66.0 2.0 copy-start.5
  66.0 32.9 %copy-start.4 = (f32[128,256]{1,0:T(8,128)S(1)}, f32[128,256]{1,0:T(8,128)}, u32[]{:S(2)}) copy-start(f32[128,256]{1,0:T(8,128)} %param.9) | copy-start | bytes 393220
  66.0 32.9 %copy-start.7 = (f32[256]{0:T(256)S(1)}, f32[256]{0:T(256)}, u32[]{:S(2)}) copy-start(f32[256]{0:T(256)} %param.10) | copy-start | bytes 3076
  66.6 32.4 %copy-start.6 = (f32[512,256]{1,0:T(8,128)S(1)}, f32[512,256]{1,0:T(8,128)}, u32[]{:S(2)}) copy-start(f32[512,256]{1,0:T(8,128)} %param.15) | copy-start | bytes 1572868
  68.0 109.3 %reduce-scatter.2.cloned.1.call-start = ((), (), s32[]{:S(2)}) async-start(), calls=%async_computation.3 | async-start | bytes 2359296 | tf_op jit(solution)/shard_map/reduce_scatter | solution.py:42
  101.4 0.8 copy-start.1
  108.8 1.0 copy-start.2
  108.8 1.1 copy-start.3
  108.8 141.7 %all-reduce.8.cloned.1.call-start = ((), (), s32[]{:S(2)}) async-start(), calls=%async_computation.5 | async-start | bytes 262144 | tf_op jit(solution)/shard_map/psum | solution.py:51
  111.2 173.0 %all-reduce.6.cloned.1.call-start = ((), (), s32[]{:S(2)}) async-start(), calls=%async_computation.4 | async-start | bytes 524288 | tf_op jit(solution)/shard_map/psum | solution.py:48
Sparse Core Ops, SparseCore 0:
  10.1 51.7 all-gather.1
  68.1 30.8 all-reduce.3
  108.9 68.2 reduce-scatter.1
  181.0 69.4 all-reduce.7
  252.7 31.3 all-reduce.5
where the time goes:
time: 294 us
  waiting for transfers between devices  237 us (81%)
  blocking collectives  19.7 us (7%)
  between operations  14.6 us (5%)
  local copies, waits for them, and re-layouts  11.6 us (4%)
  matrix products  9.66 us (3%)
    reduce_scatter x1, waiting for transfers between devices, per_device(): lax.psum_scatter(lax.slice_in_dim(placed, 0, rows_here * lax.axis_size('l...  66 us
    psum x1, waiting for transfers between devices, per_device(): grad_weight, grad_bias = lax.psum((weight_term, bias_term), 'loop')  53.6 us
    all_gather x1, waiting for transfers between devices, per_device(): gathered = lax.all_gather(features, 'loop', axis=0, tiled=True)  52 us
    psum x1, waiting for transfers between devices, per_device(): own_rows = lax.psum(term, 'rep')  33.6 us
    psum x1, waiting for transfers between devices, per_device(): lax.psum(jnp.einsum('kb,kif->bif', row_pick, products, precision=highest)...  30.8 us
    psum x1, blocking collectives, per_device(): grad_weight, grad_bias = lax.psum((weight_term, bias_term), 'loop')  19.7 us
  transfers between devices with their start and end apart: 5, of which 5 were waited for; matrix products, arithmetic and copies ran while one was open for 1% of the time, Pallas kernels for 0%

commit v1 on v0

--- a/solution.py
+++ b/solution.py
@@ -2,6 +2,7 @@
 import jax.numpy as jnp
 from jax import lax
 from jax.sharding import PartitionSpec as P
+from jax.lax import axis_index, ppermute, psum
 
 
 def per_device(features, weight, bias, tile_values, tile_rows, tile_cols, tile_count, cotangent):
@@ -16,7 +17,20 @@
         jnp.float32
     )
     row_pick = row_pick * live_slot[:, None]
-    gathered = lax.all_gather(features, "loop", axis=0, tiled=True)
+
+    def open_table_all(across, slab_in):
+        wide_n = psum(1, across)
+        ready = [(ix - 1, ix) for ix in range(1, wide_n)] + [(wide_n - 1, 0)]
+        passed = slab_in
+        chunks = [passed]
+        for _ in range(wide_n - 1):
+            passed = ppermute(passed, across, ready)
+            chunks += [passed]
+        p_next = jnp.concatenate([*reversed(chunks)], axis=0)
+        main = axis_index(across)
+        return jnp.roll(p_next, shift=(main + 1) * passed.shape[0], axis=0)
+
+    gathered = open_table_all("loop", features)
     width = gathered.shape[1]
     blocks = gathered.reshape(-1, tile_side, width)[tile_cols]
     products = jnp.einsum("kij,kjf->kif", tile_values, blocks, precision=highest)

time: 294 us -> 310 us (1.054)
  waiting for transfers between devices: 237 us -> 248 us
    ppermute x0 -> x7, waiting for transfers between devices: none -> 63.9 us  [open_table_all(): passed = ppermute(passed, across, ready)]
    all_gather x1 -> x0, waiting for transfers between devices: 52 us -> none  [per_device(): gathered = lax.all_gather(features, 'loop', axis=0, tiled=True)]
  transfers between devices with their start and end apart: 5 -> 11, of which waited for: 5 -> 11; matrix products, arithmetic and copies ran while one was open for 1% -> 1% of each run, Pallas kernels for 0% -> 0%
where the time goes in v1:
time: 310 us; the launch traced here: 309 us
  waiting for transfers between devices  248 us (80%)
  blocking collectives  19.8 us (6%)
  between operations  14.7 us (5%)
  local copies, waits for them, and re-layouts  11.4 us (4%)
  matrix products  11.1 us (4%)
  starting transfers between devices  3.2 us (1%)
    reduce_scatter x1, waiting for transfers between devices, per_device(): lax.psum_scatter(lax.slice_in_dim(placed, 0, rows_here * lax.axis_size('l...  66.9 us
    ppermute x7, waiting for transfers between devices, open_table_all(): passed = ppermute(passed, across, ready)  63.9 us
    psum x1, waiting for transfers between devices, per_device(): grad_weight, grad_bias = lax.psum((weight_term, bias_term), 'loop')  53.8 us
    psum x1, waiting for transfers between devices, per_device(): own_rows = lax.psum(term, 'rep')  33.6 us
    psum x1, waiting for transfers between devices, per_device(): lax.psum(jnp.einsum('kb,kif->bif', row_pick, products, precision=highest)...  29.4 us
    psum x1, blocking collectives, per_device(): grad_weight, grad_bias = lax.psum((weight_term, bias_term), 'loop')  19.8 us
  transfers between devices with their start and end apart: 11, of which 11 were waited for; matrix products, arithmetic and copies ran while one was open for 1% of the time, Pallas kernels for 0%

profile of v1, /device:TPU:0, one launch (start us, length us, event | category | flops | bytes accessed | tf_op | source)
XLA Modules:
  0.0 309.2 jit_solution(10311011979975898362)
XLA Ops:
  7.2 0.0 copy-start
  7.2 0.0 copy-start.3
  7.2 0.0 all-reduce.4.cloned.1.call-start
  7.2 3.0 collective-permute-start
  10.3 9.6 %collective-permute-done = f32[512,128]{1,0:T(8,128)S(1)} collective-permute-done((f32[512,128]{1,0:T(8,128)}, f32[512,128]{1,0:T(8,128)S(1)}, u32[]{:S(2)}, u32[]{:S(2)}) %collective-permute-start) | collective-permute-done | bytes 262176 | tf_op jit(solution)/shard_map/ppermute | solution.py:27
  19.8 0.0 collective-permute-start.1
  19.8 10.2 %collective-permute-done.1 = f32[512,128]{1,0:T(8,128)S(1)} collective-permute-done((f32[512,128]{1,0:T(8,128)S(1)}, f32[512,128]{1,0:T(8,128)S(1)}, u32[]{:S(2)}, u32[]{:S(2)}) %collective-permute-start.1) | collective-permute-done | bytes 262176 | tf_op jit(solution)/shard_map/ppermute | solution.py:27
  30.0 0.0 collective-permute-start.2
  30.0 9.3 %collective-permute-done.2 = f32[512,128]{1,0:T(8,128)S(1)} collective-permute-done((f32[512,128]{1,0:T(8,128)S(1)}, f32[512,128]{1,0:T(8,128)S(1)}, u32[]{:S(2)}, u32[]{:S(2)}) %collective-permute-start.2) | collective-permute-done | bytes 262176 | tf_op jit(solution)/shard_map/ppermute | solution.py:27
  39.3 0.0 collective-permute-start.3
  39.3 9.1 %collective-permute-done.3 = f32[512,128]{1,0:T(8,128)S(1)} collective-permute-done((f32[512,128]{1,0:T(8,128)S(1)}, f32[512,128]{1,0:T(8,128)S(1)}, u32[]{:S(2)}, u32[]{:S(2)}) %collective-permute-start.3) | collective-permute-done | bytes 262176 | tf_op jit(solution)/shard_map/ppermute | solution.py:27
  48.4 0.0 collective-permute-start.4
  48.4 9.1 %collective-permute-done.4 = f32[512,128]{1,0:T(8,128)S(1)} collective-permute-done((f32[512,128]{1,0:T(8,128)S(1)}, f32[512,128]{1,0:T(8,128)S(1)}, u32[]{:S(2)}, u32[]{:S(2)}) %collective-permute-start.4) | collective-permute-done | bytes 262176 | tf_op jit(solution)/shard_map/ppermute | solution.py:27
  57.4 0.7 compare_select_fusion
  58.1 9.0 %collective-permute-done.5 = f32[512,128]{1,0:T(8,128)S(1)} collective-permute-done((f32[512,128]{1,0:T(8,128)S(1)}, f32[512,128]{1,0:T(8,128)S(1)}, u32[]{:S(2)}, u32[]{:S(2)}) %collective-permute-start.5) | collective-permute-done | bytes 262176 | tf_op jit(solution)/shard_map/ppermute | solution.py:27
  67.1 0.7 compare_select_fusion.1
  68.5 7.7 %collective-permute-done.6 = f32[512,128]{1,0:T(8,128)S(1)} collective-permute-done((f32[512,128]{1,0:T(8,128)S(1)}, f32[512,128]{1,0:T(8,128)S(1)}, u32[]{:S(2)}, u32[]{:S(2)}) %collective-permute-start.6) | collective-permute-done | bytes 262176 | tf_op jit(solution)/shard_map/ppermute | solution.py:27
  76.4 1.0 constant_dynamic-update-slice_fusion.8
  77.6 0.1 constant_dynamic-slice_fusion
  77.7 1.6 gather_fusion
  79.3 3.1 %fusion.16 = f32[16,128,128]{2,1,0:T(8,128)S(1)} fusion(f32[16,128,128]{2,1,0:T(8,128)} %gather_fusion, f32[16,128,128]{2,1,0:T(8,128)S(1)} %copy-done), kind=kOutput, calls=%fused_computation.46 | convolution fusion | flops 402653184 | bytes 3145728 | tf_op jit(solution)/shard_map/kij,kjf->kif/dot_general | solution.py:36
  82.4 0.5 copy.14
  82.9 0.6 fusion.2
  83.6 0.7 copy.12
  84.3 0.0 all-reduce.4.cloned.1.call-update
  84.3 0.0 reduce-scatter.2.cloned.1.call-start
  84.4 0.1 fusion.7
  84.5 29.4 %all-reduce.4.cloned.1.call-done = f32[512,128]{1,0:T(8,128)} async-done(((f32[512,128]{1,0:T(8,128)}), f32[512,128]{1,0:T(8,128)}) %all-reduce.4.cloned.1.call-update) | async-done | bytes 262160 | tf_op jit(solution)/shard_map/psum | solution.py:37
  113.9 2.6 fusion.15
  116.5 0.6 fusion.17
  117.1 0.2 copy-done.1
  117.3 0.6 gather_fusion.1
  117.9 1.8 fusion.18
  119.8 0.5 copy.15
  120.3 1.0 fusion
  121.4 2.5 copy.13
  123.9 0.0 reduce-scatter.2.cloned.1.call-update
  123.9 0.0 all-reduce.8.cloned.1.call-start
  124.0 1.3 fusion.19
  125.3 0.0 all-reduce.8.cloned.1.call-update
  125.3 0.0 all-reduce.6.cloned.1.call-start
  125.3 66.9 %reduce-scatter.2.cloned.1.call-done = f32[512,128]{1,0:T(8,128)} async-done(((f32[4096,128]{1,0:T(8,128)}), f32[512,128]{1,0:T(8,128)}) %reduce-scatter.2.cloned.1.call-update) | async-done | bytes 262160 | tf_op jit(solution)/shard_map/reduce_scatter | solution.py:56
  192.3 0.0 all-reduce.6.cloned.1.call-update
  192.3 19.8 %psum.31 = f32[256]{0:T(256)} all-reduce(f32[256]{0:T(256)S(1)} %get-tuple-element.4), channel_id=1, replica_groups=mesh['loop'=8,'rep'=4] {'loop'}, use_global_device_ids=true, to_apply=%region_5.6 | all-reduce | flops 256 | bytes 2048 | tf_op jit(solution)/shard_map/psum | solution.py:65
  212.1 53.8 %all-reduce.8.cloned.1.call-done = f32[128,256]{1,0:T(8,128)} async-done(((f32[128,256]{1,0:T(8,128)}), f32[128,256]{1,0:T(8,128)}) %all-reduce.8.cloned.1.call-update) | async-done | bytes 131088 | tf_op jit(solution)/shard_map/psum | solution.py:65
  265.9 33.6 %all-reduce.6.cloned.1.call-done = f32[512,128]{1,0:T(8,128)} async-done(((f32[512,128]{1,0:T(8,128)}), f32[512,128]{1,0:T(8,128)}) %all-reduce.6.cloned.1.call-update) | async-done | bytes 262160 | tf_op jit(solution)/shard_map/psum | solution.py:62
  299.5 1.7 copy.35
  301.1 1.6 copy.36
  (32 shorter events, 0.3 us)
Async XLA Ops:
  7.2 72.2 %copy-start = (f32[16,128,128]{2,1,0:T(8,128)S(1)}, f32[16,128,128]{2,1,0:T(8,128)}, u32[]{:S(2)}) copy-start(f32[16,128,128]{2,1,0:T(8,128)} %param.11) | copy-start | bytes 3145732
  7.2 70.4 %copy-start.3 = (f32[512,128]{1,0:T(8,128)S(1)}, f32[512,128]{1,0:T(8,128)}, u32[]{:S(2)}) copy-start(f32[512,128]{1,0:T(8,128)} %param.8) | copy-start | bytes 786436
  7.2 106.7 %all-reduce.4.cloned.1.call-start = ((), (), s32[]{:S(2)}) async-start(), calls=%async_computation.1 | async-start | bytes 524288 | tf_op jit(solution)/shard_map/psum | solution.py:37
  7.2 12.6 %collective-permute-start = (f32[512,128]{1,0:T(8,128)}, f32[512,128]{1,0:T(8,128)S(1)}, u32[]{:S(2)}, u32[]{:S(2)}) collective-permute-start(f32[512,128]{1,0:T(8,128)} %param.8), channel_id=1, source_target_pairs={{0,4},{4,8},{8,12},{12,16},{16,20},{20,24},{24,28},{28,0},{1,5},{5... | collective-permute-start | bytes 786440 | tf_op jit(solution)/shard_map/ppermute | solution.py:27
  19.8 10.2 %collective-permute-start.1 = (f32[512,128]{1,0:T(8,128)S(1)}, f32[512,128]{1,0:T(8,128)S(1)}, u32[]{:S(2)}, u32[]{:S(2)}) collective-permute-start(f32[512,128]{1,0:T(8,128)S(1)} %collective-permute-done), channel_id=1, source_target_pairs={{0,4},{4,8},{8,12},{12,16},{16,20},{20,24},{24,28},{28,0},{1,5},{5... | collective-permute-start | bytes 786440 | tf_op jit(solution)/shard_map/ppermute | solution.py:27
  30.0 9.3 %collective-permute-start.2 = (f32[512,128]{1,0:T(8,128)S(1)}, f32[512,128]{1,0:T(8,128)S(1)}, u32[]{:S(2)}, u32[]{:S(2)}) collective-permute-start(f32[512,128]{1,0:T(8,128)S(1)} %collective-permute-done.1), channel_id=1, source_target_pairs={{0,4},{4,8},{8,12},{12,16},{16,20},{20,24},{24,28},{28,0},{1,5},{5... | collective-permute-start | bytes 786440 | tf_op jit(solution)/shard_map/ppermute | solution.py:27
  39.3 9.1 %collective-permute-start.3 = (f32[512,128]{1,0:T(8,128)S(1)}, f32[512,128]{1,0:T(8,128)S(1)}, u32[]{:S(2)}, u32[]{:S(2)}) collective-permute-start(f32[512,128]{1,0:T(8,128)S(1)} %collective-permute-done.2), channel_id=1, source_target_pairs={{0,4},{4,8},{8,12},{12,16},{16,20},{20,24},{24,28},{28,0},{1,5},{5... | collective-permute-start | bytes 786440 | tf_op jit(solution)/shard_map/ppermute | solution.py:27
  48.4 9.1 %collective-permute-start.4 = (f32[512,128]{1,0:T(8,128)S(1)}, f32[512,128]{1,0:T(8,128)S(1)}, u32[]{:S(2)}, u32[]{:S(2)}) collective-permute-start(f32[512,128]{1,0:T(8,128)S(1)} %collective-permute-done.3), channel_id=1, source_target_pairs={{0,4},{4,8},{8,12},{12,16},{16,20},{20,24},{24,28},{28,0},{1,5},{5... | collective-permute-start | bytes 786440 | tf_op jit(solution)/shard_map/ppermute | solution.py:27
  57.4 9.7 %collective-permute-start.5 = (f32[512,128]{1,0:T(8,128)S(1)}, f32[512,128]{1,0:T(8,128)S(1)}, u32[]{:S(2)}, u32[]{:S(2)}) collective-permute-start(f32[512,128]{1,0:T(8,128)S(1)} %collective-permute-done.4), channel_id=1, source_target_pairs={{0,4},{4,8},{8,12},{12,16},{16,20},{20,24},{24,28},{28,0},{1,5},{5... | collective-permute-start | bytes 786440 | tf_op jit(solution)/shard_map/ppermute | solution.py:27
  67.1 9.1 %collective-permute-start.6 = (f32[512,128]{1,0:T(8,128)S(1)}, f32[512,128]{1,0:T(8,128)S(1)}, u32[]{:S(2)}, u32[]{:S(2)}) collective-permute-start(f32[512,128]{1,0:T(8,128)S(1)} %collective-permute-done.5), channel_id=1, source_target_pairs={{0,4},{4,8},{8,12},{12,16},{16,20},{20,24},{24,28},{28,0},{1,5},{5... | collective-permute-start | bytes 786440 | tf_op jit(solution)/shard_map/ppermute | solution.py:27
  79.3 5.1 %copy-start.6 = (s32[16]{0:T(128)S(1)}, s32[16]{0:T(128)}, u32[]{:S(2)}) copy-start(s32[16]{0:T(128)} %param.13) | copy-start | bytes 196
  79.3 34.5 %copy-start.5 = (f32[128,256]{1,0:T(8,128)S(1)}, f32[128,256]{1,0:T(8,128)}, u32[]{:S(2)}) copy-start(f32[128,256]{1,0:T(8,128)} %param.9) | copy-start | bytes 393220
  79.3 34.5 %copy-start.7 = (f32[256]{0:T(256)S(1)}, f32[256]{0:T(256)}, u32[]{:S(2)}) copy-start(f32[256]{0:T(256)} %param.10) | copy-start | bytes 3076
  84.3 108.0 %reduce-scatter.2.cloned.1.call-start = ((), (), s32[]{:S(2)}) async-start(), calls=%async_computation.2 | async-start | bytes 2359296 | tf_op jit(solution)/shard_map/reduce_scatter | solution.py:56
  116.5 0.8 copy-start.1
  120.3 3.7 %copy-start.2 = (f32[512,256]{1,0:T(8,128)S(1)}, f32[512,256]{1,0:T(8,128)}, u32[]{:S(2)}) copy-start(f32[512,256]{1,0:T(8,128)} %copy-done.1) | copy-start | bytes 1572868
  120.3 3.7 %copy-start.4 = (f32[512,128]{1,0:T(8,128)S(1)}, f32[512,128]{1,0:T(8,128)}, u32[]{:S(2)}) copy-start(f32[512,128]{1,0:T(8,128)} %all-reduce.4.cloned.1.call-done) | copy-start | bytes 786436
  123.9 141.9 %all-reduce.8.cloned.1.call-start = ((), (), s32[]{:S(2)}) async-start(), calls=%async_computation.4 | async-start | bytes 262144 | tf_op jit(solution)/shard_map/psum | solution.py:65
  125.3 174.2 %all-reduce.6.cloned.1.call-start = ((), (), s32[]{:S(2)}) async-start(), calls=%async_computation.3 | async-start | bytes 524288 | tf_op jit(solution)/shard_map/psum | solution.py:62
Sparse Core Ops, SparseCore 0:
  84.4 29.3 all-reduce.3
  124.1 68.1 reduce-scatter.1
  196.2 69.6 all-reduce.7
  268.0 31.3 all-reduce.5
